TPU v7x, 256 devices: a whole 4x4x8 slice. The times are simulated.
256 devices in a mesh: ctx: 16 (over y, x), exp: 16 (over z, core).
Axes of the slice: x: 4, y: 4, z: 8, core: 2. Of those that a mesh axis runs over, the one named last changes fastest.
Arguments:
- tokens: bfloat16 [2048, 4096], P('ctx', 'exp'), may hold values from -6 to 6
- input_weight: bfloat16 [4096, 8192], P('ctx', 'exp'), may hold values from -0.09375 to 0.09375
- gate_weight: bfloat16 [4096, 8192], P('ctx', 'exp'), may hold values from -0.09375 to 0.09375
- conv_weight: float32 [4, 8192], P(None, 'exp'), may hold values from -3 to 3
- conv_bias: float32 [8192], P('exp'), may hold values from -3 to 3
- state_weight: bfloat16 [8192, 32], P('exp'), may hold values from -0.0078125 to 0.0078125
- step_size: float32 [2048, 8192], P('ctx', 'exp'), may hold values from 0 to 1, as said below
- skip_gain: float32 [8192], P('exp'), may hold values from 0.5 to 2
- output_weight: bfloat16 [8192, 4096], P('exp', 'ctx'), may hold values from -0.0625 to 0.0625
- norm_gain: float32 [4096], replicated, may hold values from 0.1 to 1.9
- router_weight: bfloat16 [4096, 16], replicated, may hold values from -0.09375 to 0.09375
- expert_gate: bfloat16 [16, 7168, 4096], P('exp', 'ctx'), may hold values from -0.09375 to 0.09375
- expert_up: bfloat16 [16, 7168, 4096], P('exp', 'ctx'), may hold values from -0.09375 to 0.09375
- expert_down: bfloat16 [16, 7168, 4096], P('exp', 'ctx'), may hold values from -0.0625 to 0.0625
- expert_ids: int32 [2048, 2], P(('ctx', 'exp')), may hold values from 0 to 15, all different within a row; in each aligned block of 8 rows (0 to 7, 8 to 15, ...) at most 2 rows name the same one
Outputs:
- layer_out: bfloat16 [2048, 4096], P(('ctx', 'exp'))
Inputs may be any that keep to these rules, and one draw needn't show every extreme that they name: `expert_ids`: each token names 2 different experts; in each aligned block of 8 tokens no expert is named by more than 2 tokens. `step_size`: a positive rate for each token and channel.
All inputs are finite; a program needn't handle non-finite values.
Results may differ from a plain program's by a relative error of at most 0.028.
Values may be sent and summed in bfloat16 or wider, within the bound.
A program may use at most 128 MiB of HBM per device.

v0:
```python
import jax
import jax.numpy as jnp
from jax import lax
from jax.sharding import PartitionSpec as P

STATE = 16
CONV = 4
TOP = 2
CAP = 2
precise = lax.Precision.HIGHEST


def shifted(shard, axis, by):
    devices = lax.axis_size(axis)
    pairs = [(i, i + by) for i in range(devices) if 0 <= i + by < devices]
    return lax.ppermute(shard, axis, pairs)


def causal_part(scores, decay_block, input_block):
    length = decay_block.shape[0]
    causal = (jnp.arange(length)[:, None] >= jnp.arange(length)[None, :])[:, :, None]
    distance = decay_block[:, None, :] - decay_block[None, :, :]
    weight = jnp.where(causal, jnp.exp(-jnp.where(causal, distance, 0.0)), 0.0)
    return jnp.einsum("ts,tsc,sc->tc", scores, weight, input_block, precision=precise)


def local(
    tokens,
    input_weight,
    gate_weight,
    conv_weight,
    conv_bias,
    state_weight,
    step_size,
    skip_gain,
    output_weight,
    norm_gain,
    router_weight,
    expert_gate,
    expert_up,
    expert_down,
    expert_ids,
):
    whole_stretch = lax.all_gather(tokens, "exp", axis=1, tiled=True)
    stretch_rows = whole_stretch.shape[0]
    inner_width = input_weight.shape[1]
    inner_x = jnp.dot(
        whole_stretch,
        lax.all_gather(input_weight, "ctx", axis=0, tiled=True),
        preferred_element_type=jnp.float32,
    )
    inner_z = jnp.dot(
        whole_stretch,
        lax.all_gather(gate_weight, "ctx", axis=0, tiled=True),
        preferred_element_type=jnp.float32,
    )
    inner_x = inner_x.astype(jnp.bfloat16)
    inner_z = inner_z.astype(jnp.bfloat16)
    earlier_rows = shifted(inner_x[stretch_rows - (CONV - 1) :], "ctx", 1)
    extended = jnp.concatenate([earlier_rows, inner_x], 0).astype(jnp.float32)
    filtered = jnp.broadcast_to(conv_bias[None, :], (stretch_rows, inner_width))
    for offset in range(CONV):
        filtered = (
            filtered + conv_weight[offset][None, :] * extended[offset : offset + stretch_rows]
        )
    mixer_in = jax.nn.silu(filtered).astype(jnp.bfloat16)
    mixer_wide = mixer_in.astype(jnp.float32)
    projections = lax.psum(
        jnp.dot(mixer_in, state_weight, preferred_element_type=jnp.float32), "exp"
    )
    input_gain = projections[:, :STATE]
    readout = projections[:, STATE:]
    cumulative = jnp.cumsum(step_size, 0)
    scores = jnp.dot(readout, input_gain.T, precision=precise)
    block_width = 128
    block_count = inner_width // block_width
    decay_blocks = cumulative.reshape(stretch_rows, block_count, block_width).transpose(1, 0, 2)
    incoming_slabs = mixer_wide.reshape(stretch_rows, block_count, block_width).transpose(1, 0, 2)
    inside = lax.map(
        lambda paired: causal_part(scores, paired[0], paired[1]), (decay_blocks, incoming_slabs)
    )
    inside = inside.transpose(1, 0, 2).reshape(stretch_rows, inner_width)
    total_decay = cumulative[stretch_rows - 1]
    tail_weight = jnp.exp(-(total_decay[None, :] - cumulative)) * mixer_wide
    local_end = jnp.dot(tail_weight.T, input_gain, precision=precise)
    stretch_keep = jnp.exp(-total_decay)

    def relay_step(turn_index, received):
        leaving = stretch_keep[:, None] * received + local_end
        return shifted(leaving, "ctx", 1)

    entering = lax.fori_loop(0, lax.axis_size("ctx") - 1, relay_step, jnp.zeros_like(local_end))
    carried = jnp.exp(-cumulative) * jnp.dot(readout, entering.T, precision=precise)
    mixed_state = (inside + carried + skip_gain[None, :] * mixer_wide) * jax.nn.silu(
        inner_z.astype(jnp.float32)
    )
    blender_result = mixed_state.astype(jnp.bfloat16)
    row_count = expert_ids.shape[0]
    start_row = lax.axis_index("exp") * row_count
    own_tokens = lax.dynamic_slice_in_dim(whole_stretch, start_row, row_count, 0)
    out_whole = lax.all_gather(output_weight, "ctx", axis=1, tiled=True)
    projected = lax.psum_scatter(
        jnp.dot(blender_result, out_whole, preferred_element_type=jnp.float32).astype(jnp.bfloat16),
        "exp",
        scatter_dimension=0,
        tiled=True,
    ).astype(jnp.float32)
    residual = (own_tokens.astype(jnp.float32) + projected).astype(jnp.bfloat16)
    stream = residual.astype(jnp.float32)
    normed = (
        stream
        * lax.rsqrt(jnp.mean(stream * stream, -1, keepdims=True) + 1e-05)
        * norm_gain[None, :]
    ).astype(jnp.bfloat16)
    logits = jnp.dot(normed, router_weight, preferred_element_type=jnp.float32)
    experts = router_weight.shape[1]
    expert_range = jnp.arange(experts, dtype=jnp.int32)
    chosen = expert_ids[:, :, None] == expert_range[None, None, :]
    selected_entry = jnp.sum(jnp.where(chosen, logits[:, None, :], 0.0), -1)
    shares = jax.nn.sigmoid(selected_entry - selected_entry[:, ::-1])
    flat_hits = chosen.reshape(row_count * TOP, experts).astype(jnp.int32)
    earlier_hits = jnp.cumsum(flat_hits, 0) - flat_hits
    slot_index = jnp.sum(earlier_hits * flat_hits, -1)
    target = expert_ids.reshape(-1) * CAP + slot_index
    placed = target[:, None] == jnp.arange(experts * CAP, dtype=jnp.int32)[None, :]
    placed = placed.reshape(row_count, TOP, experts * CAP)
    selector = jnp.any(placed, 1).astype(jnp.bfloat16)
    outgoing = lax.dot_general(
        selector, normed, (((0,), (0,)), ((), ())), preferred_element_type=jnp.float32
    ).astype(jnp.bfloat16)
    outgoing = outgoing.reshape(experts, CAP, -1)
    arrived = lax.all_to_all(outgoing, "exp", split_axis=0, concat_axis=0, tiled=True)
    arrived = arrived.reshape(-1, arrived.shape[2])
    gate_part = expert_gate[0]
    up_part = expert_up[0]
    down_part = expert_down[0]
    shard_rows = lax.all_gather(arrived, "ctx", axis=0, tiled=True)
    gate_value = lax.dot_general(
        shard_rows, gate_part, (((1,), (1,)), ((), ())), preferred_element_type=jnp.float32
    )
    up_value = lax.dot_general(
        shard_rows, up_part, (((1,), (1,)), ((), ())), preferred_element_type=jnp.float32
    )
    hidden = (jax.nn.silu(gate_value) * up_value).astype(jnp.bfloat16)
    partial_out = jnp.dot(hidden, down_part, preferred_element_type=jnp.float32)
    finished = lax.psum_scatter(
        partial_out.astype(jnp.bfloat16), "ctx", scatter_dimension=0, tiled=True
    )
    returned = lax.all_to_all(
        finished.reshape(experts, CAP, -1), "exp", split_axis=0, concat_axis=0, tiled=True
    )
    returned = returned.reshape(experts * CAP, -1).astype(jnp.float32)
    combine = jnp.sum(jnp.where(placed, shares[:, :, None], 0.0), 1)
    moe_out = jnp.dot(combine, returned, precision=precise)
    return (stream + moe_out).astype(jnp.bfloat16)


def solution(mesh):
    in_specs = (
        P("ctx", "exp"),
        P("ctx", "exp"),
        P("ctx", "exp"),
        P(None, "exp"),
        P("exp"),
        P("exp", None),
        P("ctx", "exp"),
        P("exp"),
        P("exp", "ctx"),
        P(),
        P(),
        P("exp", "ctx", None),
        P("exp", "ctx", None),
        P("exp", "ctx", None),
        P(("ctx", "exp"), None),
    )
    out_specs = P(("ctx", "exp"), None)
    return jax.shard_map(local, mesh=mesh, in_specs=in_specs, out_specs=out_specs, check_vma=False)
```

profile of v0, /device:TPU:1, one launch (start us, length us, event | category | flops | bytes accessed | tf_op | source)
XLA Modules:
  0.0 636.4 jit_solution(2759990935749958650)
XLA Ops:
  6.5 0.7 all-gather.6.cloned.1.call-update
  7.3 0.7 all-gather.8.cloned.1.call-update
  8.1 0.7 all-gather.10.cloned.1.call-update
  8.8 0.5 all-gather.12.cloned.1.call-update
  9.4 0.9 fusion.53
  10.2 1.2 reduce_window_sum.22
  11.5 39.5 %all-gather.6.cloned.1.call-done = bf16[128,4096]{1,0:T(8,128)(2,1)} async-done(((bf16[128,256]{1,0:T(8,128)(2,1)}), bf16[128,4096]{1,0:T(8,128)(2,1)}) %all-gather.6.cloned.1.call-update) | async-done | bytes 1048592 | tf_op jit(solution)/shard_map/all_gather | solution.py:44
  51.0 57.7 %all-gather.8.cloned.1.call-done = bf16[4096,512]{1,0:T(8,128)(2,1)} async-done(((bf16[256,512]{1,0:T(8,128)(2,1)}), bf16[4096,512]{1,0:T(8,128)(2,1)}) %all-gather.8.cloned.1.call-update) | async-done | bytes 4194320 | tf_op jit(solution)/shard_map/all_gather | solution.py:49
  108.7 3.2 convolution_convert_fusion.4
  112.0 3.1 collective-permute-start.1
  115.1 52.4 %all-gather.10.cloned.1.call-done = bf16[4096,512]{1,0:T(8,128)(2,1)} async-done(((bf16[256,512]{1,0:T(8,128)(2,1)}), bf16[4096,512]{1,0:T(8,128)(2,1)}) %all-gather.10.cloned.1.call-update) | async-done | bytes 4194320 | tf_op jit(solution)/shard_map/all_gather | solution.py:54
  167.4 2.9 fusion.30
  170.7 46.7 %psum.7 = f32[128,32]{0,1:T(8,128)S(1)} all-reduce(f32[128,32]{0,1:T(8,128)S(1)} %fusion.54), channel_id=1, replica_groups=mesh['ctx'=16,'exp'=16] {'exp'}, use_global_device_ids=true, to_apply=%region_1.2 | all-reduce | flops 4096 | bytes 32768 | tf_op jit(solution)/shard_map/psum | solution.py:68
  217.7 0.3 fusion.31
  218.1 39.1 %while.20 = (s32[]{:T(128)}, f32[4,128,128]{2,1,0:T(8,128)S(1)}, f32[4,128,128]{2,1,0:T(8,128)S(1)}, f32[4,128,128]{2,1,0:T(8,128)S(1)}, f32[128,128]{1,0:T(8,128)S(1)}, /*index=5*/s32[]{:T(128)}) while((s32[]{:T(128)}, f32[4,128,128]{2,1,0:T(8,128)S(1)}, f32[4,128,128]{2,1,0:T(8,128)S(1)}, f32[4,128,128]{2,1,0:T(8,128)S(1)}, ...), condition=%wide.region_3.4_spmd, body=%wide.region_2.3_spmd.sunk | while | flops 35667968 | bytes 688205 | solution.py:79
  218.1 9.7 %fusion.87 = f32[128,1,128]{2,1,0:T(1,128)S(1)} fusion(f32[128,128,1]{1,2,0:T(1,128)S(1)} %bitcast.88, f32[128,128]{1,0:T(8,128)S(1)} %get-tuple-element.140, f32[128,128]{1,0:T(8,128)S(1)} %get-tuple-element.141, pred[128,128]{1,0:T(8,128)(4,1)S(1)} %iota_compare_fusion.5), kind=kOutput, calls=%fused_computation.clone.1 | convolution fusion | flops 35651584 | bytes 278528 | tf_op jit(solution)/shard_map/while/body/eval_jaxpr/ts,tsc,sc->tc/dot_general | solution.py:24
  227.9 9.7 %fusion.87 = f32[128,1,128]{2,1,0:T(1,128)S(1)} fusion(f32[128,128,1]{1,2,0:T(1,128)S(1)} %bitcast.88, f32[128,128]{1,0:T(8,128)S(1)} %get-tuple-element.140, f32[128,128]{1,0:T(8,128)S(1)} %get-tuple-element.141, pred[128,128]{1,0:T(8,128)(4,1)S(1)} %iota_compare_fusion.5), kind=kOutput, calls=%fused_computation.clone.1 | convolution fusion | flops 35651584 | bytes 278528 | tf_op jit(solution)/shard_map/while/body/eval_jaxpr/ts,tsc,sc->tc/dot_general | solution.py:24
  237.6 9.7 %fusion.87 = f32[128,1,128]{2,1,0:T(1,128)S(1)} fusion(f32[128,128,1]{1,2,0:T(1,128)S(1)} %bitcast.88, f32[128,128]{1,0:T(8,128)S(1)} %get-tuple-element.140, f32[128,128]{1,0:T(8,128)S(1)} %get-tuple-element.141, pred[128,128]{1,0:T(8,128)(4,1)S(1)} %iota_compare_fusion.5), kind=kOutput, calls=%fused_computation.clone.1 | convolution fusion | flops 35651584 | bytes 278528 | tf_op jit(solution)/shard_map/while/body/eval_jaxpr/ts,tsc,sc->tc/dot_general | solution.py:24
  247.4 9.7 %fusion.87 = f32[128,1,128]{2,1,0:T(1,128)S(1)} fusion(f32[128,128,1]{1,2,0:T(1,128)S(1)} %bitcast.88, f32[128,128]{1,0:T(8,128)S(1)} %get-tuple-element.140, f32[128,128]{1,0:T(8,128)S(1)} %get-tuple-element.141, pred[128,128]{1,0:T(8,128)(4,1)S(1)} %iota_compare_fusion.5), kind=kOutput, calls=%fused_computation.clone.1 | convolution fusion | flops 35651584 | bytes 278528 | tf_op jit(solution)/shard_map/while/body/eval_jaxpr/ts,tsc,sc->tc/dot_general | solution.py:24
  257.1 90.6 %while.21 = (s32[]{:T(128)}, f32[512,16]{0,1:T(8,128)S(1)}, f32[512]{0:T(512)S(1)}, f32[512,16]{0,1:T(8,128)S(1)}, s32[]{:T(128)}) while((s32[]{:T(128)}, f32[512,16]{0,1:T(8,128)S(1)}, f32[512]{0:T(512)S(1)}, f32[512,16]{0,1:T(8,128)S(1)}, s32[]{:T(128)}) %tuple.40), condition=%wide.region_5.6_spmd, body=%wide.region_4.5_spmd.sunk | while | flops 16386 | bytes 231525 | solution.py:92
  257.2 2.7 collective-permute-start
  259.9 1.0 collective-permute-done
  260.9 3.6 collective-permute-start
  264.5 1.0 collective-permute-done
  265.5 3.6 collective-permute-start
  269.2 1.0 collective-permute-done
  270.2 4.0 collective-permute-start
  274.3 1.0 collective-permute-done
  275.3 3.7 collective-permute-start
  279.0 1.0 collective-permute-done
  280.0 5.8 collective-permute-start
  285.8 1.0 collective-permute-done
  286.8 5.7 collective-permute-start
  292.5 1.0 collective-permute-done
  293.5 5.8 collective-permute-start
  299.3 1.0 collective-permute-done
  300.3 5.8 collective-permute-start
  306.1 1.0 collective-permute-done
  307.1 5.8 collective-permute-start
  312.8 1.0 collective-permute-done
  313.8 5.8 collective-permute-start
  319.6 1.0 collective-permute-done
  320.6 5.8 collective-permute-start
  326.4 1.2 collective-permute-done
  327.6 5.6 collective-permute-start
  333.1 1.0 collective-permute-done
  334.2 5.8 collective-permute-start
  339.9 1.0 collective-permute-done
  340.9 5.8 collective-permute-start
  346.7 1.0 collective-permute-done
  347.7 0.5 fusion.29
  348.2 3.9 convolution_convert_fusion.1
  352.9 81.0 %reduce-scatter.3.cloned.1.call-done = bf16[8,4096]{1,0:T(8,128)(2,1)} async-done(((bf16[128,4096]{1,0:T(8,128)(2,1)}), bf16[8,4096]{1,0:T(8,128)(2,1)}) %reduce-scatter.3.cloned.1.call-update) | async-done | bytes 65552 | tf_op jit(solution)/shard_map/reduce_scatter | solution.py:102
  433.9 1.0 fusion.39
  435.4 19.1 %all_to_all.10 = bf16[16,2,4096]{2,1,0:T(2,128)(2,1)S(1)} all-to-all(bf16[16,2,4096]{2,1,0:T(2,128)(2,1)S(1)} %reshape.74), channel_id=1, replica_groups=mesh['ctx'=16,'exp'=16] {'exp'}, dimensions={0} | all-to-all | bytes 524288 | tf_op jit(solution)/shard_map/all_to_all | solution.py:132
  454.5 0.8 reshape.75
  455.5 53.0 %all-gather.14.cloned.1.call-done = bf16[512,4096]{1,0:T(8,128)(2,1)} async-done(((bf16[32,4096]{1,0:T(8,128)(2,1)}), bf16[512,4096]{1,0:T(8,128)(2,1)}) %all-gather.14.cloned.1.call-update) | async-done | bytes 4194320 | tf_op jit(solution)/shard_map/all_gather | solution.py:137
  508.5 5.4 fusion.18
  513.9 10.8 %convolution_convert_fusion = bf16[512,4096]{1,0:T(8,128)(2,1)} fusion(bf16[1,448,4096]{2,1,0:T(8,128)(2,1)} %param.32, bf16[512,4096]{1,0:T(8,128)(2,1)} %all-gather.14.cloned.1.call-done, bf16[1,448,4096]{2,1,0:T(8,128)(2,1)} %param.31, f32[512,448]{0,1:T(8,128)S(1)} %fusion.18), kind=kOutput, calls=%fused_computation.19 | convolution fusion | flops 3761569792 | bytes 16646144 | tf_op jit(solution)/shard_map/dot_general | solution.py:145
  524.7 81.0 %reduce-scatter.5.cloned.1.call-done = bf16[32,4096]{1,0:T(8,128)(2,1)} async-done(((bf16[512,4096]{1,0:T(8,128)(2,1)}), bf16[32,4096]{1,0:T(8,128)(2,1)}) %reduce-scatter.5.cloned.1.call-update) | async-done | bytes 262160 | tf_op jit(solution)/shard_map/reduce_scatter | solution.py:146
  605.7 1.8 reshape.76
  607.5 9.3 %all-to-all-start.1 = ((bf16[16,2,4096]{2,1,0:T(2,128)(2,1)}), bf16[16,2,4096]{2,1,0:T(2,128)(2,1)S(1)}, u32[]{:S(2)}, u32[]{:S(2)}) async-start(bf16[16,2,4096]{2,1,0:T(2,128)(2,1)} %reshape.76), calls=%async_computation.3 | async-start | bytes 524288 | tf_op jit(solution)/shard_map/all_to_all | solution.py:149
  617.3 11.2 %all-to-all-done.1 = bf16[16,2,4096]{2,1,0:T(2,128)(2,1)S(1)} async-done(((bf16[16,2,4096]{2,1,0:T(2,128)(2,1)}), bf16[16,2,4096]{2,1,0:T(2,128)(2,1)S(1)}, u32[]{:S(2)}, u32[]{:S(2)}) %all-to-all-start.1) | async-done | bytes 262176 | tf_op jit(solution)/shard_map/all_to_all | solution.py:149
  628.7 0.9 fusion.14
  (81 shorter events, 3.3 us)
Async XLA Ops:
  6.5 610.3 %copy-start = (bf16[4096,16]{0,1:T(8,128)(2,1)S(1)}, bf16[4096,16]{0,1:T(8,128)(2,1)}, u32[]{:S(2)}) copy-start(bf16[4096,16]{0,1:T(8,128)(2,1)} %param.29) | copy-start | bytes 393220
  6.5 44.5 %all-gather.6.cloned.1.call-start = ((), (), s32[]{:S(2)}) async-start(), calls=%async_computation.4 | async-start | bytes 1114112 | tf_op jit(solution)/shard_map/all_gather | solution.py:44
  7.3 101.4 %all-gather.8.cloned.1.call-start = ((), (), s32[]{:S(2)}) async-start(), calls=%async_computation.5 | async-start | bytes 4456448 | tf_op jit(solution)/shard_map/all_gather | solution.py:49
  8.0 159.4 %all-gather.10.cloned.1.call-start = ((), (), s32[]{:S(2)}) async-start(), calls=%async_computation.6 | async-start | bytes 4456448 | tf_op jit(solution)/shard_map/all_gather | solution.py:54
  8.7 339.5 %all-gather.12.cloned.1.call-start = ((), (), s32[]{:S(2)}) async-start(), calls=%async_computation.7 | async-start | bytes 4456448 | tf_op jit(solution)/shard_map/all_gather | solution.py:101
  9.3 424.6 %reduce-scatter.3.cloned.1.call-start = ((), (), s32[]{:S(2)}) async-start(), calls=%async_computation.8 | async-start | bytes 1114112 | tf_op jit(solution)/shard_map/reduce_scatter | solution.py:102
  51.0 116.5 %copy-start.1 = (bf16[128,4096]{1,0:T(8,128)(2,1)S(1)}, bf16[128,4096]{1,0:T(8,128)(2,1)}, u32[]{:S(2)}) copy-start(bf16[128,4096]{1,0:T(8,128)(2,1)} %all-gather.6.cloned.1.call-done) | copy-start | bytes 3145732
  111.9 58.5 %copy-start.5 = (f32[512]{0:T(512)S(1)}, f32[512]{0:T(512)}, u32[]{:S(2)}) copy-start(f32[512]{0:T(512)} %param.23) | copy-start | bytes 6148
  111.9 58.7 %copy-start.2 = (bf16[512,32]{0,1:T(8,128)(2,1)S(1)}, bf16[512,32]{0,1:T(8,128)(2,1)}, u32[]{:S(2)}) copy-start(bf16[512,32]{0,1:T(8,128)(2,1)} %param.24) | copy-start | bytes 98308
  112.0 58.4 %collective-permute-start.1 = (bf16[3,512]{1,0:T(4,128)(2,1)S(1)}, bf16[3,512]{1,0:T(4,128)(2,1)S(1)}, u32[]{:S(2)}, u32[]{:S(2)}) collective-permute-start(bf16[3,512]{1,0:T(4,128)(2,1)S(1)} %slice.48), channel_id=1, source_target_pairs={{0,16},{16,32},{32,48},{48,64},{64,80},{80,96},{96,112},{112,128},... | collective-permute-start | bytes 9224 | tf_op jit(solution)/shard_map/ppermute | solution.py:16
  218.1 129.7 %copy-start.6 = (f32[512]{0:T(512)S(1)}, f32[512]{0:T(512)}, u32[]{:S(2)}) copy-start(f32[512]{0:T(512)} %param.26) | copy-start | bytes 6148
  257.2 3.7 collective-permute-start
  260.9 4.7 collective-permute-start
  265.5 4.7 collective-permute-start
  270.2 5.1 collective-permute-start
  275.3 4.7 collective-permute-start
  280.0 6.9 %collective-permute-start = (f32[512,16]{0,1:T(8,128)S(1)}, f32[512,16]{0,1:T(8,128)S(1)}, u32[]{:S(2)}, u32[]{:S(2)}) collective-permute-start(f32[512,16]{0,1:T(8,128)S(1)} %multiply_add_fusion.3), channel_id=1, source_target_pairs={{0,16},{16,32},{32,48},{48,64},{64,80},{80,96},{96,112},{112,128},... | collective-permute-start | bytes 98312 | tf_op jit(solution)/shard_map/while/body/eval_jaxpr/ppermute | solution.py:16
  286.8 6.7 %collective-permute-start = (f32[512,16]{0,1:T(8,128)S(1)}, f32[512,16]{0,1:T(8,128)S(1)}, u32[]{:S(2)}, u32[]{:S(2)}) collective-permute-start(f32[512,16]{0,1:T(8,128)S(1)} %multiply_add_fusion.3), channel_id=1, source_target_pairs={{0,16},{16,32},{32,48},{48,64},{64,80},{80,96},{96,112},{112,128},... | collective-permute-start | bytes 98312 | tf_op jit(solution)/shard_map/while/body/eval_jaxpr/ppermute | solution.py:16
  293.5 6.8 %collective-permute-start = (f32[512,16]{0,1:T(8,128)S(1)}, f32[512,16]{0,1:T(8,128)S(1)}, u32[]{:S(2)}, u32[]{:S(2)}) collective-permute-start(f32[512,16]{0,1:T(8,128)S(1)} %multiply_add_fusion.3), channel_id=1, source_target_pairs={{0,16},{16,32},{32,48},{48,64},{64,80},{80,96},{96,112},{112,128},... | collective-permute-start | bytes 98312 | tf_op jit(solution)/shard_map/while/body/eval_jaxpr/ppermute | solution.py:16
  300.3 6.8 %collective-permute-start = (f32[512,16]{0,1:T(8,128)S(1)}, f32[512,16]{0,1:T(8,128)S(1)}, u32[]{:S(2)}, u32[]{:S(2)}) collective-permute-start(f32[512,16]{0,1:T(8,128)S(1)} %multiply_add_fusion.3), channel_id=1, source_target_pairs={{0,16},{16,32},{32,48},{48,64},{64,80},{80,96},{96,112},{112,128},... | collective-permute-start | bytes 98312 | tf_op jit(solution)/shard_map/while/body/eval_jaxpr/ppermute | solution.py:16
  307.1 6.8 %collective-permute-start = (f32[512,16]{0,1:T(8,128)S(1)}, f32[512,16]{0,1:T(8,128)S(1)}, u32[]{:S(2)}, u32[]{:S(2)}) collective-permute-start(f32[512,16]{0,1:T(8,128)S(1)} %multiply_add_fusion.3), channel_id=1, source_target_pairs={{0,16},{16,32},{32,48},{48,64},{64,80},{80,96},{96,112},{112,128},... | collective-permute-start | bytes 98312 | tf_op jit(solution)/shard_map/while/body/eval_jaxpr/ppermute | solution.py:16
  313.8 6.8 %collective-permute-start = (f32[512,16]{0,1:T(8,128)S(1)}, f32[512,16]{0,1:T(8,128)S(1)}, u32[]{:S(2)}, u32[]{:S(2)}) collective-permute-start(f32[512,16]{0,1:T(8,128)S(1)} %multiply_add_fusion.3), channel_id=1, source_target_pairs={{0,16},{16,32},{32,48},{48,64},{64,80},{80,96},{96,112},{112,128},... | collective-permute-start | bytes 98312 | tf_op jit(solution)/shard_map/while/body/eval_jaxpr/ppermute | solution.py:16
  320.6 6.9 %collective-permute-start = (f32[512,16]{0,1:T(8,128)S(1)}, f32[512,16]{0,1:T(8,128)S(1)}, u32[]{:S(2)}, u32[]{:S(2)}) collective-permute-start(f32[512,16]{0,1:T(8,128)S(1)} %multiply_add_fusion.3), channel_id=1, source_target_pairs={{0,16},{16,32},{32,48},{48,64},{64,80},{80,96},{96,112},{112,128},... | collective-permute-start | bytes 98312 | tf_op jit(solution)/shard_map/while/body/eval_jaxpr/ppermute | solution.py:16
  327.6 6.6 %collective-permute-start = (f32[512,16]{0,1:T(8,128)S(1)}, f32[512,16]{0,1:T(8,128)S(1)}, u32[]{:S(2)}, u32[]{:S(2)}) collective-permute-start(f32[512,16]{0,1:T(8,128)S(1)} %multiply_add_fusion.3), channel_id=1, source_target_pairs={{0,16},{16,32},{32,48},{48,64},{64,80},{80,96},{96,112},{112,128},... | collective-permute-start | bytes 98312 | tf_op jit(solution)/shard_map/while/body/eval_jaxpr/ppermute | solution.py:16
  334.2 6.8 %collective-permute-start = (f32[512,16]{0,1:T(8,128)S(1)}, f32[512,16]{0,1:T(8,128)S(1)}, u32[]{:S(2)}, u32[]{:S(2)}) collective-permute-start(f32[512,16]{0,1:T(8,128)S(1)} %multiply_add_fusion.3), channel_id=1, source_target_pairs={{0,16},{16,32},{32,48},{48,64},{64,80},{80,96},{96,112},{112,128},... | collective-permute-start | bytes 98312 | tf_op jit(solution)/shard_map/while/body/eval_jaxpr/ppermute | solution.py:16
  340.9 6.8 %collective-permute-start = (f32[512,16]{0,1:T(8,128)S(1)}, f32[512,16]{0,1:T(8,128)S(1)}, u32[]{:S(2)}, u32[]{:S(2)}) collective-permute-start(f32[512,16]{0,1:T(8,128)S(1)} %multiply_add_fusion.3), channel_id=1, source_target_pairs={{0,16},{16,32},{32,48},{48,64},{64,80},{80,96},{96,112},{112,128},... | collective-permute-start | bytes 98312 | tf_op jit(solution)/shard_map/while/body/eval_jaxpr/ppermute | solution.py:16
  347.7 4.5 copy-start.4
  347.7 87.2 %copy-start.3 = (f32[4096]{0:T(1024)S(1)}, f32[4096]{0:T(1024)}, u32[]{:S(2)}) copy-start(f32[4096]{0:T(1024)} %param.28) | copy-start | bytes 49156
  352.1 156.4 %all-gather.14.cloned.1.call-start = ((), (), s32[]{:S(2)}) async-start(), calls=%async_computation.9 | async-start | bytes 4456448 | tf_op jit(solution)/shard_map/all_gather | solution.py:137
  455.3 150.4 %reduce-scatter.5.cloned.1.call-start = ((), (), s32[]{:S(2)}) async-start(), calls=%async_computation.10 | async-start | bytes 4456448 | tf_op jit(solution)/shard_map/reduce_scatter | solution.py:146
  607.5 21.1 %all-to-all-start.1 = ((bf16[16,2,4096]{2,1,0:T(2,128)(2,1)}), bf16[16,2,4096]{2,1,0:T(2,128)(2,1)S(1)}, u32[]{:S(2)}, u32[]{:S(2)}) async-start(bf16[16,2,4096]{2,1,0:T(2,128)(2,1)} %reshape.76), calls=%async_computation.3 | async-start | bytes 524288 | tf_op jit(solution)/shard_map/all_to_all | solution.py:149
Sparse Core Ops, SparseCore 0:
  9.1 41.8 all-gather.5
  53.4 55.2 all-gather.7
  111.1 56.2 all-gather.9
  169.7 61.4 all-gather.11
  352.2 81.6 reduce-scatter.2
  455.4 53.0 all-gather.13
  524.8 80.7 reduce-scatter.4
where the time goes:
time: 637 us; the launch traced here: 636 us
  waiting for transfers between devices  394 us (62%)
  starting transfers between devices  87.9 us (14%)
  matrix products  67.4 us (11%)
  blocking collectives  65.7 us (10%)
  between operations  13.7 us (2%)
    reduce_scatter x1, waiting for transfers between devices, local(): lax.psum_scatter(jnp.dot(blender_result, out_whole, preferred_element_typ...  81 us
    reduce_scatter x1, waiting for transfers between devices, local(): lax.psum_scatter(partial_out.astype(jnp.bfloat16), 'ctx', scatter_dimensi...  81 us
    ppermute x16, starting transfers between devices, shifted(): return lax.ppermute(shard, axis, pairs)  78.2 us
    all_gather x1, waiting for transfers between devices, local(): lax.all_gather(input_weight, 'ctx', axis=0, tiled=True)  57.7 us
    all_gather x1, waiting for transfers between devices, local(): shard_rows = lax.all_gather(arrived, 'ctx', axis=0, tiled=True)  53 us
    all_gather x1, waiting for transfers between devices, local(): lax.all_gather(gate_weight, 'ctx', axis=0, tiled=True)  52.4 us
    psum x1, blocking collectives, local(): lax.psum(jnp.dot(mixer_in, state_weight, preferred_element_type=jnp.float...  46.7 us
    all_gather x1, waiting for transfers between devices, local(): whole_stretch = lax.all_gather(tokens, 'exp', axis=1, tiled=True)  39.5 us
  transfers between devices with their start and end apart: 24, of which 22 were waited for; matrix products, arithmetic and copies ran while one was open for 8% of the time, Pallas kernels for 0%

commit v1 on v0

--- a/solution.py
+++ b/solution.py
@@ -1,3 +1,4 @@
+import functools
 import jax
 import jax.numpy as jnp
 from jax import lax
@@ -8,6 +9,14 @@
 TOP = 2
 CAP = 2
 precise = lax.Precision.HIGHEST
+
+
+def serve_the_face(payload, bus_axis):
+    seen_now = lax.all_gather(payload, bus_axis)
+    return jnp.sum(seen_now, axis=0)
+
+
+create_samples_on = functools.partial(serve_the_face, bus_axis="exp")
 
 
 def shifted(shard, axis, by):
@@ -65,8 +74,8 @@
         )
     mixer_in = jax.nn.silu(filtered).astype(jnp.bfloat16)
     mixer_wide = mixer_in.astype(jnp.float32)
-    projections = lax.psum(
-        jnp.dot(mixer_in, state_weight, preferred_element_type=jnp.float32), "exp"
+    projections = create_samples_on(
+        jnp.dot(mixer_in, state_weight, preferred_element_type=jnp.float32)
     )
     input_gain = projections[:, :STATE]
     readout = projections[:, STATE:]

time: 637 us -> 606 us (0.951)
  blocking collectives: 65.7 us -> 37.8 us
    psum x1 -> x0, blocking collectives: 46.7 us -> none  [local(): lax.psum(jnp.dot(mixer_in, state_weight, preferred_element_type=jnp.float...]
    all_gather x0 -> x1, blocking collectives: none -> 18.7 us  [serve_the_face(): seen_now = lax.all_gather(payload, bus_axis)]
where the time goes in v1:
time: 606 us
  waiting for transfers between devices  391 us (65%)
  starting transfers between devices  88 us (15%)
  matrix products  67.4 us (11%)
  blocking collectives  37.8 us (6%)
  between operations  13.7 us (2%)
    reduce_scatter x1, waiting for transfers between devices, local(): lax.psum_scatter(partial_out.astype(jnp.bfloat16), 'ctx', scatter_dimensi...  80.9 us
    ppermute x16, starting transfers between devices, shifted(): return lax.ppermute(shard, axis, pairs)  78.3 us
    reduce_scatter x1, waiting for transfers between devices, local(): lax.psum_scatter(jnp.dot(blender_result, out_whole, preferred_element_typ...  77.7 us
    all_gather x1, waiting for transfers between devices, local(): lax.all_gather(input_weight, 'ctx', axis=0, tiled=True)  57.7 us
    all_gather x1, waiting for transfers between devices, local(): shard_rows = lax.all_gather(arrived, 'ctx', axis=0, tiled=True)  53.1 us
    all_gather x1, waiting for transfers between devices, local(): lax.all_gather(gate_weight, 'ctx', axis=0, tiled=True)  52.4 us
    all_gather x1, waiting for transfers between devices, local(): whole_stretch = lax.all_gather(tokens, 'exp', axis=1, tiled=True)  39.5 us
    dot_general x4, matrix products, causal_part(): jnp.einsum('ts,tsc,sc->tc', scores, weight, input_block, precision=precise)  38.7 us
  transfers between devices with their start and end apart: 24, of which 22 were waited for; matrix products, arithmetic and copies ran while one was open for 8% of the time, Pallas kernels for 0%

profile of v1, /device:TPU:1, one launch (start us, length us, event | category | flops | bytes accessed | tf_op | source)
XLA Modules:
  0.0 605.5 jit_solution(11083080969810667060)
XLA Ops:
  6.5 0.7 all-gather.7.cloned.1.call-update
  7.3 0.7 all-gather.9.cloned.1.call-update
  8.1 0.7 all-gather.11.cloned.1.call-update
  8.8 0.5 all-gather.13.cloned.1.call-update
  9.4 1.2 reduce_window_sum.22
  10.6 0.9 fusion.53
  11.5 39.5 %all-gather.7.cloned.1.call-done = bf16[128,4096]{1,0:T(8,128)(2,1)} async-done(((bf16[128,256]{1,0:T(8,128)(2,1)}), bf16[128,4096]{1,0:T(8,128)(2,1)}) %all-gather.7.cloned.1.call-update) | async-done | bytes 1048592 | tf_op jit(solution)/shard_map/all_gather | solution.py:53
  51.0 57.7 %all-gather.9.cloned.1.call-done = bf16[4096,512]{1,0:T(8,128)(2,1)} async-done(((bf16[256,512]{1,0:T(8,128)(2,1)}), bf16[4096,512]{1,0:T(8,128)(2,1)}) %all-gather.9.cloned.1.call-update) | async-done | bytes 4194320 | tf_op jit(solution)/shard_map/all_gather | solution.py:58
  108.7 3.2 convolution_convert_fusion.4
  112.0 3.1 collective-permute-start.1
  115.1 52.4 %all-gather.11.cloned.1.call-done = bf16[4096,512]{1,0:T(8,128)(2,1)} async-done(((bf16[256,512]{1,0:T(8,128)(2,1)}), bf16[4096,512]{1,0:T(8,128)(2,1)}) %all-gather.11.cloned.1.call-update) | async-done | bytes 4194320 | tf_op jit(solution)/shard_map/all_gather | solution.py:63
  167.4 2.9 fusion.30
  170.7 18.7 %all-gather = f32[2048,32]{0,1:T(8,128)S(1)} all-gather(f32[128,32]{0,1:T(8,128)S(1)} %fusion.54), channel_id=2, replica_groups=mesh['ctx'=16,'exp'=16] {'exp'}, dimensions={0}, use_global_device_ids=true | all-gather | bytes 278528 | tf_op jit(solution)/shard_map/all_gather | solution.py:15
  189.8 0.3 fusion.31
  190.1 39.1 %while.20 = (s32[]{:T(128)}, f32[4,128,128]{2,1,0:T(8,128)S(1)}, f32[4,128,128]{2,1,0:T(8,128)S(1)}, f32[4,128,128]{2,1,0:T(8,128)S(1)}, f32[128,128]{1,0:T(8,128)S(1)}, /*index=5*/s32[]{:T(128)}) while((s32[]{:T(128)}, f32[4,128,128]{2,1,0:T(8,128)S(1)}, f32[4,128,128]{2,1,0:T(8,128)S(1)}, f32[4,128,128]{2,1,0:T(8,128)S(1)}, ...), condition=%wide.region_3.4_spmd, body=%wide.region_2.3_spmd.sunk | while | flops 35667968 | bytes 688205 | solution.py:88
  190.2 9.7 %fusion.87 = f32[128,1,128]{2,1,0:T(1,128)S(1)} fusion(f32[128,128,1]{1,2,0:T(1,128)S(1)} %bitcast.97, f32[128,128]{1,0:T(8,128)S(1)} %get-tuple-element.138, f32[128,128]{1,0:T(8,128)S(1)} %get-tuple-element.139, pred[128,128]{1,0:T(8,128)(4,1)S(1)} %iota_compare_fusion.5), kind=kOutput, calls=%fused_computation.clone.1 | convolution fusion | flops 35651584 | bytes 278528 | tf_op jit(solution)/shard_map/while/body/eval_jaxpr/ts,tsc,sc->tc/dot_general | solution.py:33
  200.0 9.7 %fusion.87 = f32[128,1,128]{2,1,0:T(1,128)S(1)} fusion(f32[128,128,1]{1,2,0:T(1,128)S(1)} %bitcast.97, f32[128,128]{1,0:T(8,128)S(1)} %get-tuple-element.138, f32[128,128]{1,0:T(8,128)S(1)} %get-tuple-element.139, pred[128,128]{1,0:T(8,128)(4,1)S(1)} %iota_compare_fusion.5), kind=kOutput, calls=%fused_computation.clone.1 | convolution fusion | flops 35651584 | bytes 278528 | tf_op jit(solution)/shard_map/while/body/eval_jaxpr/ts,tsc,sc->tc/dot_general | solution.py:33
  209.7 9.7 %fusion.87 = f32[128,1,128]{2,1,0:T(1,128)S(1)} fusion(f32[128,128,1]{1,2,0:T(1,128)S(1)} %bitcast.97, f32[128,128]{1,0:T(8,128)S(1)} %get-tuple-element.138, f32[128,128]{1,0:T(8,128)S(1)} %get-tuple-element.139, pred[128,128]{1,0:T(8,128)(4,1)S(1)} %iota_compare_fusion.5), kind=kOutput, calls=%fused_computation.clone.1 | convolution fusion | flops 35651584 | bytes 278528 | tf_op jit(solution)/shard_map/while/body/eval_jaxpr/ts,tsc,sc->tc/dot_general | solution.py:33
  219.5 9.7 %fusion.87 = f32[128,1,128]{2,1,0:T(1,128)S(1)} fusion(f32[128,128,1]{1,2,0:T(1,128)S(1)} %bitcast.97, f32[128,128]{1,0:T(8,128)S(1)} %get-tuple-element.138, f32[128,128]{1,0:T(8,128)S(1)} %get-tuple-element.139, pred[128,128]{1,0:T(8,128)(4,1)S(1)} %iota_compare_fusion.5), kind=kOutput, calls=%fused_computation.clone.1 | convolution fusion | flops 35651584 | bytes 278528 | tf_op jit(solution)/shard_map/while/body/eval_jaxpr/ts,tsc,sc->tc/dot_general | solution.py:33
  229.2 90.8 %while.21 = (s32[]{:T(128)}, f32[512,16]{0,1:T(8,128)S(1)}, f32[512]{0:T(512)S(1)}, f32[512,16]{0,1:T(8,128)S(1)}, s32[]{:T(128)}) while((s32[]{:T(128)}, f32[512,16]{0,1:T(8,128)S(1)}, f32[512]{0:T(512)S(1)}, f32[512,16]{0,1:T(8,128)S(1)}, s32[]{:T(128)}) %tuple.39), condition=%wide.region_5.6_spmd, body=%wide.region_4.5_spmd.sunk | while | flops 16386 | bytes 231525 | solution.py:101
  229.2 3.1 collective-permute-start
  232.3 1.0 collective-permute-done
  233.4 3.6 collective-permute-start
  237.0 1.0 collective-permute-done
  238.0 3.6 collective-permute-start
  241.7 1.0 collective-permute-done
  242.7 3.6 collective-permute-start
  246.3 1.0 collective-permute-done
  247.3 3.7 collective-permute-start
  251.1 1.0 collective-permute-done
  252.1 5.8 collective-permute-start
  257.9 1.0 collective-permute-done
  258.9 5.8 collective-permute-start
  264.6 1.0 collective-permute-done
  265.6 5.8 collective-permute-start
  271.4 1.1 collective-permute-done
  272.5 5.7 collective-permute-start
  278.2 1.0 collective-permute-done
  279.2 5.8 collective-permute-start
  284.9 1.0 collective-permute-done
  285.9 5.8 collective-permute-start
  291.7 1.0 collective-permute-done
  292.7 5.8 collective-permute-start
  298.5 1.0 collective-permute-done
  299.5 5.8 collective-permute-start
  305.3 1.0 collective-permute-done
  306.3 5.8 collective-permute-start
  312.0 1.0 collective-permute-done
  313.0 5.8 collective-permute-start
  318.8 1.2 collective-permute-done
  320.0 0.5 fusion.29
  320.5 3.9 convolution_convert_fusion.1
  325.2 77.7 %reduce-scatter.3.cloned.1.call-done = bf16[8,4096]{1,0:T(8,128)(2,1)} async-done(((bf16[128,4096]{1,0:T(8,128)(2,1)}), bf16[8,4096]{1,0:T(8,128)(2,1)}) %reduce-scatter.3.cloned.1.call-update) | async-done | bytes 65552 | tf_op jit(solution)/shard_map/reduce_scatter | solution.py:111
  402.9 1.0 fusion.39
  404.4 19.1 %all_to_all.10 = bf16[16,2,4096]{2,1,0:T(2,128)(2,1)S(1)} all-to-all(bf16[16,2,4096]{2,1,0:T(2,128)(2,1)S(1)} %reshape.74), channel_id=1, replica_groups=mesh['ctx'=16,'exp'=16] {'exp'}, dimensions={0} | all-to-all | bytes 524288 | tf_op jit(solution)/shard_map/all_to_all | solution.py:141
  423.5 0.8 reshape.75
  424.6 53.1 %all-gather.15.cloned.1.call-done = bf16[512,4096]{1,0:T(8,128)(2,1)} async-done(((bf16[32,4096]{1,0:T(8,128)(2,1)}), bf16[512,4096]{1,0:T(8,128)(2,1)}) %all-gather.15.cloned.1.call-update) | async-done | bytes 4194320 | tf_op jit(solution)/shard_map/all_gather | solution.py:146
  477.7 5.4 fusion.18
  483.1 10.8 %convolution_convert_fusion = bf16[512,4096]{1,0:T(8,128)(2,1)} fusion(bf16[1,448,4096]{2,1,0:T(8,128)(2,1)} %param.32, bf16[512,4096]{1,0:T(8,128)(2,1)} %all-gather.15.cloned.1.call-done, bf16[1,448,4096]{2,1,0:T(8,128)(2,1)} %param.31, f32[512,448]{0,1:T(8,128)S(1)} %fusion.18), kind=kOutput, calls=%fused_computation.19 | convolution fusion | flops 3761569792 | bytes 16646144 | tf_op jit(solution)/shard_map/dot_general | solution.py:154
  493.9 80.9 %reduce-scatter.5.cloned.1.call-done = bf16[32,4096]{1,0:T(8,128)(2,1)} async-done(((bf16[512,4096]{1,0:T(8,128)(2,1)}), bf16[32,4096]{1,0:T(8,128)(2,1)}) %reduce-scatter.5.cloned.1.call-update) | async-done | bytes 262160 | tf_op jit(solution)/shard_map/reduce_scatter | solution.py:155
  574.8 1.8 reshape.76
  576.6 9.4 %all-to-all-start.1 = ((bf16[16,2,4096]{2,1,0:T(2,128)(2,1)}), bf16[16,2,4096]{2,1,0:T(2,128)(2,1)S(1)}, u32[]{:S(2)}, u32[]{:S(2)}) async-start(bf16[16,2,4096]{2,1,0:T(2,128)(2,1)} %reshape.76), calls=%async_computation.3 | async-start | bytes 524288 | tf_op jit(solution)/shard_map/all_to_all | solution.py:158
  586.5 11.2 %all-to-all-done.1 = bf16[16,2,4096]{2,1,0:T(2,128)(2,1)S(1)} async-done(((bf16[16,2,4096]{2,1,0:T(2,128)(2,1)}), bf16[16,2,4096]{2,1,0:T(2,128)(2,1)S(1)}, u32[]{:S(2)}, u32[]{:S(2)}) %all-to-all-start.1) | async-done | bytes 262176 | tf_op jit(solution)/shard_map/all_to_all | solution.py:158
  597.8 0.9 fusion.14
  (84 shorter events, 3.3 us)
Async XLA Ops:
  6.5 579.5 %copy-start = (bf16[4096,16]{0,1:T(8,128)(2,1)S(1)}, bf16[4096,16]{0,1:T(8,128)(2,1)}, u32[]{:S(2)}) copy-start(bf16[4096,16]{0,1:T(8,128)(2,1)} %param.29) | copy-start | bytes 393220
  6.5 44.5 %all-gather.7.cloned.1.call-start = ((), (), s32[]{:S(2)}) async-start(), calls=%async_computation.4 | async-start | bytes 1114112 | tf_op jit(solution)/shard_map/all_gather | solution.py:53
  7.3 101.4 %all-gather.9.cloned.1.call-start = ((), (), s32[]{:S(2)}) async-start(), calls=%async_computation.5 | async-start | bytes 4456448 | tf_op jit(solution)/shard_map/all_gather | solution.py:58
  8.0 159.4 %all-gather.11.cloned.1.call-start = ((), (), s32[]{:S(2)}) async-start(), calls=%async_computation.6 | async-start | bytes 4456448 | tf_op jit(solution)/shard_map/all_gather | solution.py:63
  8.7 311.8 %all-gather.13.cloned.1.call-start = ((), (), s32[]{:S(2)}) async-start(), calls=%async_computation.7 | async-start | bytes 4456448 | tf_op jit(solution)/shard_map/all_gather | solution.py:110
  9.3 393.6 %reduce-scatter.3.cloned.1.call-start = ((), (), s32[]{:S(2)}) async-start(), calls=%async_computation.8 | async-start | bytes 1114112 | tf_op jit(solution)/shard_map/reduce_scatter | solution.py:111
  51.0 116.5 %copy-start.1 = (bf16[128,4096]{1,0:T(8,128)(2,1)S(1)}, bf16[128,4096]{1,0:T(8,128)(2,1)}, u32[]{:S(2)}) copy-start(bf16[128,4096]{1,0:T(8,128)(2,1)} %all-gather.7.cloned.1.call-done) | copy-start | bytes 3145732
  111.9 58.5 %copy-start.5 = (f32[512]{0:T(512)S(1)}, f32[512]{0:T(512)}, u32[]{:S(2)}) copy-start(f32[512]{0:T(512)} %param.23) | copy-start | bytes 6148
  111.9 58.7 %copy-start.2 = (bf16[512,32]{0,1:T(8,128)(2,1)S(1)}, bf16[512,32]{0,1:T(8,128)(2,1)}, u32[]{:S(2)}) copy-start(bf16[512,32]{0,1:T(8,128)(2,1)} %param.24) | copy-start | bytes 98308
  112.0 58.4 %collective-permute-start.1 = (bf16[3,512]{1,0:T(4,128)(2,1)S(1)}, bf16[3,512]{1,0:T(4,128)(2,1)S(1)}, u32[]{:S(2)}, u32[]{:S(2)}) collective-permute-start(bf16[3,512]{1,0:T(4,128)(2,1)S(1)} %slice.48), channel_id=1, source_target_pairs={{0,16},{16,32},{32,48},{48,64},{64,80},{80,96},{96,112},{112,128},... | collective-permute-start | bytes 9224 | tf_op jit(solution)/shard_map/ppermute | solution.py:25
  190.1 129.9 %copy-start.6 = (f32[512]{0:T(512)S(1)}, f32[512]{0:T(512)}, u32[]{:S(2)}) copy-start(f32[512]{0:T(512)} %param.26) | copy-start | bytes 6148
  229.2 4.1 collective-permute-start
  233.4 4.7 collective-permute-start
  238.0 4.7 collective-permute-start
  242.7 4.7 collective-permute-start
  247.3 4.7 collective-permute-start
  252.1 6.8 %collective-permute-start = (f32[512,16]{0,1:T(8,128)S(1)}, f32[512,16]{0,1:T(8,128)S(1)}, u32[]{:S(2)}, u32[]{:S(2)}) collective-permute-start(f32[512,16]{0,1:T(8,128)S(1)} %multiply_add_fusion.3), channel_id=1, source_target_pairs={{0,16},{16,32},{32,48},{48,64},{64,80},{80,96},{96,112},{112,128},... | collective-permute-start | bytes 98312 | tf_op jit(solution)/shard_map/while/body/eval_jaxpr/ppermute | solution.py:25
  258.9 6.8 %collective-permute-start = (f32[512,16]{0,1:T(8,128)S(1)}, f32[512,16]{0,1:T(8,128)S(1)}, u32[]{:S(2)}, u32[]{:S(2)}) collective-permute-start(f32[512,16]{0,1:T(8,128)S(1)} %multiply_add_fusion.3), channel_id=1, source_target_pairs={{0,16},{16,32},{32,48},{48,64},{64,80},{80,96},{96,112},{112,128},... | collective-permute-start | bytes 98312 | tf_op jit(solution)/shard_map/while/body/eval_jaxpr/ppermute | solution.py:25
  265.6 6.8 %collective-permute-start = (f32[512,16]{0,1:T(8,128)S(1)}, f32[512,16]{0,1:T(8,128)S(1)}, u32[]{:S(2)}, u32[]{:S(2)}) collective-permute-start(f32[512,16]{0,1:T(8,128)S(1)} %multiply_add_fusion.3), channel_id=1, source_target_pairs={{0,16},{16,32},{32,48},{48,64},{64,80},{80,96},{96,112},{112,128},... | collective-permute-start | bytes 98312 | tf_op jit(solution)/shard_map/while/body/eval_jaxpr/ppermute | solution.py:25
  272.5 6.7 %collective-permute-start = (f32[512,16]{0,1:T(8,128)S(1)}, f32[512,16]{0,1:T(8,128)S(1)}, u32[]{:S(2)}, u32[]{:S(2)}) collective-permute-start(f32[512,16]{0,1:T(8,128)S(1)} %multiply_add_fusion.3), channel_id=1, source_target_pairs={{0,16},{16,32},{32,48},{48,64},{64,80},{80,96},{96,112},{112,128},... | collective-permute-start | bytes 98312 | tf_op jit(solution)/shard_map/while/body/eval_jaxpr/ppermute | solution.py:25
  279.2 6.8 %collective-permute-start = (f32[512,16]{0,1:T(8,128)S(1)}, f32[512,16]{0,1:T(8,128)S(1)}, u32[]{:S(2)}, u32[]{:S(2)}) collective-permute-start(f32[512,16]{0,1:T(8,128)S(1)} %multiply_add_fusion.3), channel_id=1, source_target_pairs={{0,16},{16,32},{32,48},{48,64},{64,80},{80,96},{96,112},{112,128},... | collective-permute-start | bytes 98312 | tf_op jit(solution)/shard_map/while/body/eval_jaxpr/ppermute | solution.py:25
  285.9 6.8 %collective-permute-start = (f32[512,16]{0,1:T(8,128)S(1)}, f32[512,16]{0,1:T(8,128)S(1)}, u32[]{:S(2)}, u32[]{:S(2)}) collective-permute-start(f32[512,16]{0,1:T(8,128)S(1)} %multiply_add_fusion.3), channel_id=1, source_target_pairs={{0,16},{16,32},{32,48},{48,64},{64,80},{80,96},{96,112},{112,128},... | collective-permute-start | bytes 98312 | tf_op jit(solution)/shard_map/while/body/eval_jaxpr/ppermute | solution.py:25
  292.7 6.8 %collective-permute-start = (f32[512,16]{0,1:T(8,128)S(1)}, f32[512,16]{0,1:T(8,128)S(1)}, u32[]{:S(2)}, u32[]{:S(2)}) collective-permute-start(f32[512,16]{0,1:T(8,128)S(1)} %multiply_add_fusion.3), channel_id=1, source_target_pairs={{0,16},{16,32},{32,48},{48,64},{64,80},{80,96},{96,112},{112,128},... | collective-permute-start | bytes 98312 | tf_op jit(solution)/shard_map/while/body/eval_jaxpr/ppermute | solution.py:25
  299.5 6.8 %collective-permute-start = (f32[512,16]{0,1:T(8,128)S(1)}, f32[512,16]{0,1:T(8,128)S(1)}, u32[]{:S(2)}, u32[]{:S(2)}) collective-permute-start(f32[512,16]{0,1:T(8,128)S(1)} %multiply_add_fusion.3), channel_id=1, source_target_pairs={{0,16},{16,32},{32,48},{48,64},{64,80},{80,96},{96,112},{112,128},... | collective-permute-start | bytes 98312 | tf_op jit(solution)/shard_map/while/body/eval_jaxpr/ppermute | solution.py:25
  306.3 6.8 %collective-permute-start = (f32[512,16]{0,1:T(8,128)S(1)}, f32[512,16]{0,1:T(8,128)S(1)}, u32[]{:S(2)}, u32[]{:S(2)}) collective-permute-start(f32[512,16]{0,1:T(8,128)S(1)} %multiply_add_fusion.3), channel_id=1, source_target_pairs={{0,16},{16,32},{32,48},{48,64},{64,80},{80,96},{96,112},{112,128},... | collective-permute-start | bytes 98312 | tf_op jit(solution)/shard_map/while/body/eval_jaxpr/ppermute | solution.py:25
  313.0 6.9 %collective-permute-start = (f32[512,16]{0,1:T(8,128)S(1)}, f32[512,16]{0,1:T(8,128)S(1)}, u32[]{:S(2)}, u32[]{:S(2)}) collective-permute-start(f32[512,16]{0,1:T(8,128)S(1)} %multiply_add_fusion.3), channel_id=1, source_target_pairs={{0,16},{16,32},{32,48},{48,64},{64,80},{80,96},{96,112},{112,128},... | collective-permute-start | bytes 98312 | tf_op jit(solution)/shard_map/while/body/eval_jaxpr/ppermute | solution.py:25
  320.0 4.5 copy-start.4
  320.0 83.9 %copy-start.3 = (f32[4096]{0:T(1024)S(1)}, f32[4096]{0:T(1024)}, u32[]{:S(2)}) copy-start(f32[4096]{0:T(1024)} %param.28) | copy-start | bytes 49156
  324.4 153.3 %all-gather.15.cloned.1.call-start = ((), (), s32[]{:S(2)}) async-start(), calls=%async_computation.9 | async-start | bytes 4456448 | tf_op jit(solution)/shard_map/all_gather | solution.py:146
  424.3 150.5 %reduce-scatter.5.cloned.1.call-start = ((), (), s32[]{:S(2)}) async-start(), calls=%async_computation.10 | async-start | bytes 4456448 | tf_op jit(solution)/shard_map/reduce_scatter | solution.py:155
  576.6 21.1 %all-to-all-start.1 = ((bf16[16,2,4096]{2,1,0:T(2,128)(2,1)}), bf16[16,2,4096]{2,1,0:T(2,128)(2,1)S(1)}, u32[]{:S(2)}, u32[]{:S(2)}) async-start(bf16[16,2,4096]{2,1,0:T(2,128)(2,1)} %reshape.76), calls=%async_computation.3 | async-start | bytes 524288 | tf_op jit(solution)/shard_map/all_to_all | solution.py:158
Sparse Core Ops, SparseCore 0:
  9.1 41.8 all-gather.6
  53.4 55.2 all-gather.8
  111.1 56.2 all-gather.10
  169.7 61.4 all-gather.12
  324.5 78.3 reduce-scatter.2
  424.5 53.1 all-gather.14
  494.0 80.7 reduce-scatter.4
